TPU v7x, 512 devices: a whole 4x4x16 slice. The times are simulated.
512 devices in a mesh: gx: 32 (over x, y, core), gy: 16 (over z).
Axes of the slice: x: 4, y: 4, z: 16, core: 2. Of those that a mesh axis runs over, the one named last changes fastest.
Arguments:
- conductance: float32 [16, 256, 2048], P(None, 'gx', 'gy'), may hold values from 0.2 to 5
- labels: int32 [16, 256, 2048], P(None, 'gx', 'gy'), may hold values from 0 to 2, as said below
- cotangent: float32 [2, 16, 256, 2048], P(None, None, 'gx', 'gy')
- saved: float32 [2, 16, 256, 2048], P(None, None, 'gx', 'gy'), may hold values from 0 to 1
Outputs:
- adjoint: float32 [2, 16, 256, 2048], P(None, None, 'gx', 'gy')
- gradient: float32 [16, 256, 2048], P(None, 'gx', 'gy')
Inputs may be any that keep to these rules, and one draw needn't show every extreme that they name: `labels`: 0 marks an unseeded voxel, 1 or 2 the class of a seed.
All inputs are finite; a program needn't handle non-finite values.
Results may differ from a plain program's by a relative error of at most 0.0003.
Values sent between devices are 32-bit elements; how exact they have to be, the bound alone decides.
No kernel may reach another device: no remote copies, remote signals or barrier semaphores. Data moves between devices by JAX's collectives and lax.ppermute only.
A program may use at most 64 MiB of HBM per device.

v0:
```python
import jax
import jax.numpy as jnp
from jax import lax
from jax.sharding import PartitionSpec as P

ITERS = 3
prior_strength = 1.0


def extended(x, sides, width):
    for axis, dim in sides:
        size, length = (lax.axis_size(axis), x.shape[dim])
        up = [(i, (i + 1) % size) for i in range(size - 1)]
        down = [(j, i) for i, j in up]
        last = lax.slice_in_dim(x, length - width, length, axis=dim)
        initial = lax.slice_in_dim(x, 0, width, axis=dim)
        before = lax.ppermute(last, axis, up)
        after = lax.ppermute(initial, axis, down)
        x = jnp.concatenate([before, x, after], axis=dim)
    return x


def potentials(labels, saved):
    classes = jnp.arange(1, 3, dtype=jnp.int32)[:, None, None, None]
    tagged = labels[None]
    return jnp.where(tagged == classes, 1.0, jnp.where(tagged > 0, 0.0, saved))


def edge_validity(row_count, col_count, depth):
    row_pos = lax.axis_index("gx") * row_count + jnp.arange(row_count, dtype=jnp.int32)
    col_pos = lax.axis_index("gy") * col_count + jnp.arange(col_count, dtype=jnp.int32)
    depth_pos = jnp.arange(depth, dtype=jnp.int32)
    total_rows = row_count * lax.axis_size("gx")
    total_cols = col_count * lax.axis_size("gy")
    return (
        (row_pos > 0).astype(jnp.float32)[None, :, None],
        (row_pos < total_rows - 1).astype(jnp.float32)[None, :, None],
        (col_pos > 0).astype(jnp.float32)[None, None, :],
        (col_pos < total_cols - 1).astype(jnp.float32)[None, None, :],
        (depth_pos > 0).astype(jnp.float32)[:, None, None],
        (depth_pos < depth - 1).astype(jnp.float32)[:, None, None],
    )


def side_slices(padded):
    return (
        padded[..., :-2, 1:-1],
        padded[..., 2:, 1:-1],
        padded[..., 1:-1, :-2],
        padded[..., 1:-1, 2:],
    )


def depth_neighbours(input_vector):
    depth_axis = input_vector.ndim - 3
    depth = input_vector.shape[depth_axis]
    widths = [(0, 0)] * input_vector.ndim
    widths[depth_axis] = (1, 1)
    padded = jnp.pad(input_vector, widths)
    lower = lax.slice_in_dim(padded, 0, depth, axis=depth_axis)
    upper = lax.slice_in_dim(padded, 2, depth + 2, axis=depth_axis)
    return (lower, upper)


def apply_operator(input_vector, unlabelled_mask, weight_field):
    mask_applied = unlabelled_mask * input_vector
    padded = extended(mask_applied, (("gx", 2), ("gy", 3)), 1)
    neighbours = side_slices(padded) + depth_neighbours(mask_applied)
    graph_laplacian = jnp.zeros_like(mask_applied)
    for weight, neighbour in zip(weight_field, neighbours):
        graph_laplacian = graph_laplacian + weight * (mask_applied - neighbour)
    return (
        unlabelled_mask * (prior_strength * mask_applied + graph_laplacian)
        + (1.0 - unlabelled_mask) * input_vector
    )


def class_sum(first_vec, second_vec):
    return jnp.sum(first_vec * second_vec, axis=(1, 2, 3))


def expand(scalars):
    return scalars[:, None, None, None]


def global_norm(solver_residual):
    return lax.psum(class_sum(solver_residual, solver_residual), ("gx", "gy"))


def per_device(conductance, labels, cotangent, saved):
    depth, row_count, col_count = conductance.shape
    validity = edge_validity(row_count, col_count, depth)
    potential = potentials(labels, saved)
    unlabelled_mask = (labels == 0).astype(jnp.float32)[None]
    solver_residual = unlabelled_mask * cotangent
    cond_pad = extended(conductance, (("gx", 1), ("gy", 2)), 1)
    cond_neighbours = side_slices(cond_pad) + depth_neighbours(conductance)
    weight_field = [
        0.5 * (conductance + neighbour) * valid_edge
        for neighbour, valid_edge in zip(cond_neighbours, validity)
    ]
    adjoint = jnp.zeros_like(solver_residual)
    search_direction = solver_residual
    norm_now = global_norm(solver_residual)
    for iteration in range(ITERS):
        operator_result = apply_operator(search_direction, unlabelled_mask, weight_field)
        step_size = norm_now / lax.psum(class_sum(search_direction, operator_result), ("gx", "gy"))
        adjoint = adjoint + expand(step_size) * search_direction
        solver_residual = solver_residual - expand(step_size) * operator_result
        if iteration + 1 < ITERS:
            norm_next = global_norm(solver_residual)
            search_direction = solver_residual + expand(norm_next / norm_now) * search_direction
            norm_now = norm_next
    joined = extended(jnp.concatenate((adjoint, potential), axis=0), (("gx", 2), ("gy", 3)), 1)
    adj_pad = joined[:2]
    pot_pad = joined[2:]
    adj_neighbours = side_slices(adj_pad) + depth_neighbours(adjoint)
    pot_neighbours = side_slices(pot_pad) + depth_neighbours(potential)
    gradient = jnp.zeros_like(conductance)
    for adj_nb, pot_nb, valid_edge in zip(adj_neighbours, pot_neighbours, validity):
        gradient = (
            gradient - jnp.sum((adjoint - adj_nb) * (potential - pot_nb), axis=0) * valid_edge
        )
    return (adjoint, 0.5 * gradient)


def solution(mesh):
    return jax.shard_map(
        per_device,
        mesh=mesh,
        in_specs=(
            P(None, "gx", "gy"),
            P(None, "gx", "gy"),
            P(None, None, "gx", "gy"),
            P(None, None, "gx", "gy"),
        ),
        out_specs=(P(None, None, "gx", "gy"), P(None, "gx", "gy")),
        check_vma=False,
    )
```

profile of v0, /device:TPU:1, one launch (start us, length us, event | category | flops | bytes accessed | tf_op | source)
XLA Modules:
  0.0 619.8 jit_solution(12101957498100516942)
XLA Ops:
  0.6 0.9 broadcast_compare_fusion
  1.5 0.0 copy-done.1
  1.6 0.0 copy-start.2
  1.6 4.7 collective-permute-start.1
  6.4 5.5 collective-permute-start.3
  11.9 1.9 collective-permute-start
  13.8 2.4 collective-permute-start.2
  16.3 0.1 fusion.83
  16.4 0.0 collective-permute-done
  16.4 2.4 collective-permute-done.2
  18.8 0.1 fusion.102
  18.9 1.7 collective-permute-start.4
  20.6 1.3 collective-permute-start.6
  21.9 0.0 collective-permute-done.1
  21.9 0.1 pad_maximum_fusion.1
  22.0 0.1 fusion.99
  22.1 4.2 collective-permute-start.5
  26.3 1.3 collective-permute-start.7
  27.7 0.2 fusion.89
  27.8 3.5 collective-permute-done.5
  31.4 4.1 collective-permute-done.7
  35.5 0.4 multiply_reduce_fusion.3
  35.9 112.1 %all-reduce.6 = (f32[2]{0:T(128)S(1)}, f32[2]{0:T(128)S(1)}) all-reduce(f32[2]{0:T(128)S(1)} %get-tuple-element.9, f32[2]{0:T(128)S(1)} %get-tuple-element.8), channel_id=1, replica_groups=mesh['gx'=32,'gy'=16] {'gx','gy'}, use_global_device_ids=true, to_apply=%region_1.2 | all-reduce | flops 4 | bytes 32 | tf_op jit(solution)/shard_map/psum | solution.py:87
  148.0 0.2 multiply_reduce_fusion.2
  148.2 98.7 %psum.44 = f32[2]{0:T(128)S(1)} all-reduce(f32[2]{0:T(128)S(1)} %get-tuple-element.18), channel_id=1, replica_groups=mesh['gx'=32,'gy'=16] {'gx','gy'}, use_global_device_ids=true, to_apply=%region_5.6 | all-reduce | flops 2 | bytes 16 | tf_op jit(solution)/shard_map/psum | solution.py:87
  246.8 0.1 broadcast_multiply_fusion.1
  246.9 3.4 collective-permute-start.8
  250.4 1.9 collective-permute-start.9
  252.3 3.1 collective-permute-done.9
  255.5 0.1 fusion.98
  255.6 3.7 collective-permute-start.10
  259.3 1.3 collective-permute-start.11
  260.6 3.3 collective-permute-done.10
  263.9 4.1 collective-permute-done.11
  268.0 0.3 multiply_reduce_fusion.1
  268.4 101.5 %psum.45 = f32[2]{0:T(128)S(1)} all-reduce(f32[2]{0:T(128)S(1)} %get-tuple-element.14), channel_id=1, replica_groups=mesh['gx'=32,'gy'=16] {'gx','gy'}, use_global_device_ids=true, to_apply=%region_7.8 | all-reduce | flops 2 | bytes 16 | tf_op jit(solution)/shard_map/psum | solution.py:107
  369.9 0.2 multiply_reduce_fusion
  370.1 99.5 %psum.46 = f32[2]{0:T(128)S(1)} all-reduce(f32[2]{0:T(128)S(1)} %multiply_reduce_fusion), channel_id=1, replica_groups=mesh['gx'=32,'gy'=16] {'gx','gy'}, use_global_device_ids=true, to_apply=%region_9.10 | all-reduce | flops 2 | bytes 16 | tf_op jit(solution)/shard_map/psum | solution.py:87
  469.6 0.1 broadcast_multiply_fusion
  469.7 3.5 collective-permute-start.12
  473.2 1.9 collective-permute-start.13
  475.2 0.1 select_select_fusion
  475.3 3.0 collective-permute-done.13
  478.4 0.1 fusion.97
  478.5 3.7 collective-permute-start.14
  482.2 1.3 collective-permute-start.15
  483.5 3.3 collective-permute-done.14
  486.8 4.1 collective-permute-done.15
  490.9 0.4 fusion.81
  491.3 101.5 %psum.47 = f32[2]{0:T(128)S(1)} all-reduce(f32[2]{0:T(128)S(1)} %fusion.81), channel_id=1, replica_groups=mesh['gx'=32,'gy'=16] {'gx','gy'}, use_global_device_ids=true, to_apply=%region_11.12 | all-reduce | flops 2 | bytes 16 | tf_op jit(solution)/shard_map/psum | solution.py:107
  592.7 0.1 multiply_add_fusion
  592.8 0.0 copy-start
  592.9 3.7 collective-permute-start.16
  596.6 1.9 collective-permute-start.17
  598.6 3.3 collective-permute-done.17
  601.9 0.1 pad_maximum_fusion
  602.0 0.2 fusion.96
  602.2 2.4 collective-permute-start.18
  604.6 1.3 collective-permute-start.19
  605.9 8.7 %collective-permute-done.18 = f32[4,16,10,1]{3,2,1,0:T(8,128)S(1)} collective-permute-done((f32[4,16,10,1]{3,2,1,0:T(8,128)S(1)}, f32[4,16,10,1]{3,2,1,0:T(8,128)S(1)}, u32[]{:S(2)}, u32[]{:S(2)}) %collective-permute-start.18) | collective-permute-done | bytes 2592 | tf_op jit(solution)/shard_map/ppermute | solution.py:17
  614.6 0.2 fusion.44
  614.8 4.0 collective-permute-done.19
  618.8 0.3 fusion.47
  619.1 0.7 subtract_multiply_fusion
  (36 shorter events, 0.4 us)
Async XLA Ops:
  0.6 0.9 copy-start.1
  1.6 14.7 %copy-start.3 = (s32[16,8,128]{2,1,0:T(8,128)S(1)}, s32[16,8,128]{2,1,0:T(8,128)}, u32[]{:S(2)}) copy-start(s32[16,8,128]{2,1,0:T(8,128)} %param.5) | copy-start | bytes 196612
  1.6 10.3 %copy-start.2 = (f32[16,8,128]{2,1,0:T(8,128)S(1)}, f32[16,8,128]{2,1,0:T(8,128)}, u32[]{:S(2)}) copy-start(f32[16,8,128]{2,1,0:T(8,128)} %param.4) | copy-start | bytes 196612
  1.6 20.3 %collective-permute-start.1 = (f32[2,16,1,128]{3,2,1,0:T(1,128)S(1)}, f32[2,16,1,128]{3,2,1,0:T(1,128)S(1)}, u32[]{:S(2)}, u32[]{:S(2)}) collective-permute-start(f32[2,16,1,128]{3,2,1,0:T(1,128)S(1)} %get-tuple-element.37), channel_id=1, source_target_pairs={{0,16},{16,32},{32,48},{48,64},{64,80},{80,96},{96,112},{112,128},... | collective-permute-start | bytes 49160 | tf_op jit(solution)/shard_map/ppermute | solution.py:17
  6.4 15.6 %collective-permute-start.3 = (f32[2,16,1,128]{3,2,1,0:T(1,128)S(1)}, f32[2,16,1,128]{3,2,1,0:T(1,128)S(1)}, u32[]{:S(2)}, u32[]{:S(2)}) collective-permute-start(f32[2,16,1,128]{3,2,1,0:T(1,128)S(1)} %get-tuple-element.38), channel_id=1, source_target_pairs={{16,0},{32,16},{48,32},{64,48},{80,64},{96,80},{112,96},{128,112},... | collective-permute-start | bytes 49160 | tf_op jit(solution)/shard_map/ppermute | solution.py:18
  11.9 4.5 collective-permute-start
  13.8 5.0 collective-permute-start.2
  18.9 8.7 %collective-permute-start.4 = (f32[16,10,1]{2,1,0:T(8,128)S(1)}, f32[16,10,1]{2,1,0:T(8,128)S(1)}, u32[]{:S(2)}, u32[]{:S(2)}) collective-permute-start(f32[16,10,1]{2,1,0:T(8,128)S(1)} %get-tuple-element.35), channel_id=1, source_target_pairs={{0,1},{1,2},{2,3},{3,4},{4,5},{5,6},{6,7},{7,8},{8,9},{9,10},{10,1... | collective-permute-start | bytes 1928 | tf_op jit(solution)/shard_map/ppermute | solution.py:17
  20.6 7.0 %collective-permute-start.6 = (f32[16,10,1]{2,1,0:T(8,128)S(1)}, f32[16,10,1]{2,1,0:T(8,128)S(1)}, u32[]{:S(2)}, u32[]{:S(2)}) collective-permute-start(f32[16,10,1]{2,1,0:T(8,128)S(1)} %get-tuple-element.36), channel_id=1, source_target_pairs={{1,0},{2,1},{3,2},{4,3},{5,4},{6,5},{7,6},{8,7},{9,8},{10,9},{11,1... | collective-permute-start | bytes 1928 | tf_op jit(solution)/shard_map/ppermute | solution.py:18
  22.1 9.2 %collective-permute-start.5 = (f32[2,16,10,1]{3,2,1,0:T(8,128)S(1)}, f32[2,16,10,1]{3,2,1,0:T(8,128)S(1)}, u32[]{:S(2)}, u32[]{:S(2)}) collective-permute-start(f32[2,16,10,1]{3,2,1,0:T(8,128)S(1)} %get-tuple-element.29), channel_id=1, source_target_pairs={{0,1},{1,2},{2,3},{3,4},{4,5},{5,6},{6,7},{7,8},{8,9},{9,10},{10,1... | collective-permute-start | bytes 3848 | tf_op jit(solution)/shard_map/ppermute | solution.py:17
  26.3 9.2 %collective-permute-start.7 = (f32[2,16,10,1]{3,2,1,0:T(8,128)S(1)}, f32[2,16,10,1]{3,2,1,0:T(8,128)S(1)}, u32[]{:S(2)}, u32[]{:S(2)}) collective-permute-start(f32[2,16,10,1]{3,2,1,0:T(8,128)S(1)} %get-tuple-element.30), channel_id=1, source_target_pairs={{1,0},{2,1},{3,2},{4,3},{5,4},{6,5},{7,6},{8,7},{9,8},{10,9},{11,1... | collective-permute-start | bytes 3848 | tf_op jit(solution)/shard_map/ppermute | solution.py:18
  246.9 5.4 collective-permute-start.8
  250.4 5.1 collective-permute-start.9
  255.6 8.3 %collective-permute-start.10 = (f32[2,16,10,1]{3,2,1,0:T(8,128)S(1)}, f32[2,16,10,1]{3,2,1,0:T(8,128)S(1)}, u32[]{:S(2)}, u32[]{:S(2)}) collective-permute-start(f32[2,16,10,1]{3,2,1,0:T(8,128)S(1)} %get-tuple-element.27), channel_id=1, source_target_pairs={{0,1},{1,2},{2,3},{3,4},{4,5},{5,6},{6,7},{7,8},{8,9},{9,10},{10,1... | collective-permute-start | bytes 3848 | tf_op jit(solution)/shard_map/ppermute | solution.py:17
  259.3 8.7 %collective-permute-start.11 = (f32[2,16,10,1]{3,2,1,0:T(8,128)S(1)}, f32[2,16,10,1]{3,2,1,0:T(8,128)S(1)}, u32[]{:S(2)}, u32[]{:S(2)}) collective-permute-start(f32[2,16,10,1]{3,2,1,0:T(8,128)S(1)} %get-tuple-element.28), channel_id=1, source_target_pairs={{1,0},{2,1},{3,2},{4,3},{5,4},{6,5},{7,6},{8,7},{9,8},{10,9},{11,1... | collective-permute-start | bytes 3848 | tf_op jit(solution)/shard_map/ppermute | solution.py:18
  469.6 5.6 copy-start.4
  469.7 5.5 collective-permute-start.12
  473.2 5.1 collective-permute-start.13
  478.5 8.3 %collective-permute-start.14 = (f32[2,16,10,1]{3,2,1,0:T(8,128)S(1)}, f32[2,16,10,1]{3,2,1,0:T(8,128)S(1)}, u32[]{:S(2)}, u32[]{:S(2)}) collective-permute-start(f32[2,16,10,1]{3,2,1,0:T(8,128)S(1)} %get-tuple-element.25), channel_id=1, source_target_pairs={{0,1},{1,2},{2,3},{3,4},{4,5},{5,6},{6,7},{7,8},{8,9},{9,10},{10,1... | collective-permute-start | bytes 3848 | tf_op jit(solution)/shard_map/ppermute | solution.py:17
  482.2 8.7 %collective-permute-start.15 = (f32[2,16,10,1]{3,2,1,0:T(8,128)S(1)}, f32[2,16,10,1]{3,2,1,0:T(8,128)S(1)}, u32[]{:S(2)}, u32[]{:S(2)}) collective-permute-start(f32[2,16,10,1]{3,2,1,0:T(8,128)S(1)} %get-tuple-element.26), channel_id=1, source_target_pairs={{1,0},{2,1},{3,2},{4,3},{5,4},{6,5},{7,6},{8,7},{9,8},{10,9},{11,1... | collective-permute-start | bytes 3848 | tf_op jit(solution)/shard_map/ppermute | solution.py:18
  592.8 26.0 %copy-start = (f32[2,16,8,128]{3,2,1,0:T(8,128)}, f32[2,16,8,128]{3,2,1,0:T(8,128)S(1)}, u32[]{:S(2)}) copy-start(f32[2,16,8,128]{3,2,1,0:T(8,128)S(1)} %multiply_add_fusion) | copy-start | bytes 393220
  592.9 5.7 collective-permute-start.16
  596.6 5.2 collective-permute-start.17
  602.2 12.5 %collective-permute-start.18 = (f32[4,16,10,1]{3,2,1,0:T(8,128)S(1)}, f32[4,16,10,1]{3,2,1,0:T(8,128)S(1)}, u32[]{:S(2)}, u32[]{:S(2)}) collective-permute-start(f32[4,16,10,1]{3,2,1,0:T(8,128)S(1)} %get-tuple-element.21), channel_id=1, source_target_pairs={{0,1},{1,2},{2,3},{3,4},{4,5},{5,6},{6,7},{7,8},{8,9},{9,10},{10,1... | collective-permute-start | bytes 7688 | tf_op jit(solution)/shard_map/ppermute | solution.py:17
  604.6 14.2 %collective-permute-start.19 = (f32[4,16,10,1]{3,2,1,0:T(8,128)S(1)}, f32[4,16,10,1]{3,2,1,0:T(8,128)S(1)}, u32[]{:S(2)}, u32[]{:S(2)}) collective-permute-start(f32[4,16,10,1]{3,2,1,0:T(8,128)S(1)} %get-tuple-element.22), channel_id=1, source_target_pairs={{1,0},{2,1},{3,2},{4,3},{5,4},{6,5},{7,6},{8,7},{9,8},{10,9},{11,1... | collective-permute-start | bytes 7688 | tf_op jit(solution)/shard_map/ppermute | solution.py:18
where the time goes:
time: 621 us; the launch traced here: 620 us
  blocking collectives  513 us (83%)
  starting transfers between devices  53.1 us (9%)
  waiting for transfers between devices  46.9 us (8%)
    psum x3, blocking collectives, global_norm(): return lax.psum(class_sum(solver_residual, solver_residual), ('gx', 'gy'))  310 us
    psum x2, blocking collectives, per_device(): lax.psum(class_sum(search_direction, operator_result), ('gx', 'gy'))  203 us
    ppermute x10, starting transfers between devices, extended(): before = lax.ppermute(last, axis, up)  33 us
    ppermute x10, waiting for transfers between devices, extended(): after = lax.ppermute(initial, axis, down)  28.1 us
    ppermute x10, starting transfers between devices, extended(): after = lax.ppermute(initial, axis, down)  20.1 us
    ppermute x10, waiting for transfers between devices, extended(): before = lax.ppermute(last, axis, up)  18.8 us
  transfers between devices with their start and end apart: 20, of which 12 were waited for; matrix products, arithmetic and copies ran while one was open for 0% of the time, Pallas kernels for 0%

commit v1 on v0

--- a/solution.py
+++ b/solution.py
@@ -104,7 +104,13 @@
     norm_now = global_norm(solver_residual)
     for iteration in range(ITERS):
         operator_result = apply_operator(search_direction, unlabelled_mask, weight_field)
-        step_size = norm_now / lax.psum(class_sum(search_direction, operator_result), ("gx", "gy"))
+
+        def post_run(load, ax_name, mesh_dim):
+            for kk in (ax_name, mesh_dim):
+                load = jax.lax.psum(load, kk)
+            return load
+
+        step_size = norm_now / post_run(class_sum(search_direction, operator_result), "gy", "gx")
         adjoint = adjoint + expand(step_size) * search_direction
         solver_residual = solver_residual - expand(step_size) * operator_result
         if iteration + 1 < ITERS:

time: 621 us -> 682 us (1.098)
  blocking collectives: 513 us -> 580 us
    psum x2 -> x6, blocking collectives: 203 us -> 281 us  [post_run(): load = jax.lax.psum(load, kk)]
    psum x3, blocking collectives: 310 us -> 298 us  [global_norm(): return lax.psum(class_sum(solver_residual, solver_residual), ('gx', 'gy'))]
where the time goes in v1:
time: 682 us; the launch traced here: 680 us
  blocking collectives  580 us (85%)
  starting transfers between devices  47.2 us (7%)
  waiting for transfers between devices  46.9 us (7%)
    psum x3, blocking collectives, global_norm(): return lax.psum(class_sum(solver_residual, solver_residual), ('gx', 'gy'))  298 us
    psum x6, blocking collectives, post_run(): load = jax.lax.psum(load, kk)  281 us
    ppermute x10, waiting for transfers between devices, extended(): after = lax.ppermute(initial, axis, down)  27.5 us
    ppermute x10, starting transfers between devices, extended(): before = lax.ppermute(last, axis, up)  26.4 us
    ppermute x10, starting transfers between devices, extended(): after = lax.ppermute(initial, axis, down)  20.8 us
    ppermute x10, waiting for transfers between devices, extended(): before = lax.ppermute(last, axis, up)  19.4 us
  transfers between devices with their start and end apart: 20, of which 12 were waited for; matrix products, arithmetic and copies ran while one was open for 0% of the time, Pallas kernels for 0%

profile of v1, /device:TPU:1, one launch (start us, length us, event | category | flops | bytes accessed | tf_op | source)
XLA Modules:
  0.0 680.2 jit_solution(550349070228046635)
XLA Ops:
  0.6 0.9 broadcast_compare_fusion
  1.5 0.0 copy-done.1
  1.6 4.7 collective-permute-start.1
  6.4 5.5 collective-permute-start.3
  11.9 1.9 collective-permute-start
  13.8 2.4 collective-permute-start.2
  16.3 0.1 fusion.83
  16.4 2.4 collective-permute-done.2
  18.8 0.1 fusion.102
  18.9 1.7 collective-permute-start.4
  20.6 1.3 collective-permute-start.6
  21.9 0.1 pad_maximum_fusion.1
  22.0 0.1 fusion.99
  22.1 4.2 collective-permute-start.5
  26.3 1.3 collective-permute-start.7
  27.7 0.2 fusion.89
  27.8 3.5 collective-permute-done.5
  31.4 4.1 collective-permute-done.7
  35.5 0.4 multiply_reduce_fusion.3
  35.9 30.1 %psum.64 = f32[2]{0:T(128)S(1)} all-reduce(f32[2]{0:T(128)S(1)} %get-tuple-element.8), channel_id=1, replica_groups=mesh['gx'=32,'gy'=16] {'gy'}, use_global_device_ids=true, to_apply=%region_3.4 | all-reduce | flops 2 | bytes 16 | tf_op jit(solution)/shard_map/psum | solution.py:110
  66.0 68.8 %psum.65 = f32[2]{0:T(128)S(1)} all-reduce(f32[2]{0:T(128)S(1)} %psum.64), channel_id=1, replica_groups=mesh['gx'=32,'gy'=16] {'gx'}, use_global_device_ids=true, to_apply=%region_4.5 | all-reduce | flops 2 | bytes 16 | tf_op jit(solution)/shard_map/psum | solution.py:110
  134.8 98.7 %psum.63 = f32[2]{0:T(128)S(1)} all-reduce(f32[2]{0:T(128)S(1)} %get-tuple-element.9), channel_id=1, replica_groups=mesh['gx'=32,'gy'=16] {'gx','gy'}, use_global_device_ids=true, to_apply=%region_1.2 | all-reduce | flops 2 | bytes 16 | tf_op jit(solution)/shard_map/psum | solution.py:87
  233.5 0.2 multiply_reduce_fusion.2
  233.7 100.7 %psum.66 = f32[2]{0:T(128)S(1)} all-reduce(f32[2]{0:T(128)S(1)} %get-tuple-element.16), channel_id=1, replica_groups=mesh['gx'=32,'gy'=16] {'gx','gy'}, use_global_device_ids=true, to_apply=%region_6.7 | all-reduce | flops 2 | bytes 16 | tf_op jit(solution)/shard_map/psum | solution.py:87
  334.4 0.1 broadcast_multiply_fusion.1
  334.5 2.9 collective-permute-start.8
  337.4 1.9 collective-permute-start.9
  339.4 3.1 collective-permute-done.9
  342.5 0.1 fusion.98
  342.7 1.8 collective-permute-start.10
  344.5 1.3 collective-permute-start.11
  345.8 3.3 collective-permute-done.10
  349.0 4.1 collective-permute-done.11
  353.2 0.3 multiply_reduce_fusion.1
  353.5 23.6 %psum.67 = f32[2]{0:T(128)S(1)} all-reduce(f32[2]{0:T(128)S(1)} %get-tuple-element.12), channel_id=1, replica_groups=mesh['gx'=32,'gy'=16] {'gy'}, use_global_device_ids=true, to_apply=%region_8.9 | all-reduce | flops 2 | bytes 16 | tf_op jit(solution)/shard_map/psum | solution.py:110
  377.1 68.0 %psum.68 = f32[2]{0:T(128)S(1)} all-reduce(f32[2]{0:T(128)S(1)} %psum.67), channel_id=1, replica_groups=mesh['gx'=32,'gy'=16] {'gx'}, use_global_device_ids=true, to_apply=%region_9.10 | all-reduce | flops 2 | bytes 16 | tf_op jit(solution)/shard_map/psum | solution.py:110
  445.0 0.2 multiply_reduce_fusion
  445.2 98.7 %psum.69 = f32[2]{0:T(128)S(1)} all-reduce(f32[2]{0:T(128)S(1)} %multiply_reduce_fusion), channel_id=1, replica_groups=mesh['gx'=32,'gy'=16] {'gx','gy'}, use_global_device_ids=true, to_apply=%region_11.12 | all-reduce | flops 2 | bytes 16 | tf_op jit(solution)/shard_map/psum | solution.py:87
  543.9 0.1 broadcast_multiply_fusion
  544.1 2.2 collective-permute-start.12
  546.3 2.1 collective-permute-start.13
  548.4 2.9 collective-permute-done.13
  551.4 0.1 fusion.97
  551.5 3.7 collective-permute-start.14
  555.2 1.3 collective-permute-start.15
  556.5 0.1 select_select_fusion
  556.6 3.4 collective-permute-done.14
  560.0 4.1 collective-permute-done.15
  564.2 0.4 fusion.81
  564.5 22.1 %psum.70 = f32[2]{0:T(128)S(1)} all-reduce(f32[2]{0:T(128)S(1)} %fusion.81), channel_id=1, replica_groups=mesh['gx'=32,'gy'=16] {'gy'}, use_global_device_ids=true, to_apply=%region_13.14 | all-reduce | flops 2 | bytes 16 | tf_op jit(solution)/shard_map/psum | solution.py:110
  586.7 68.8 %psum.71 = f32[2]{0:T(128)S(1)} all-reduce(f32[2]{0:T(128)S(1)} %psum.70), channel_id=1, replica_groups=mesh['gx'=32,'gy'=16] {'gx'}, use_global_device_ids=true, to_apply=%region_14.15 | all-reduce | flops 2 | bytes 16 | tf_op jit(solution)/shard_map/psum | solution.py:110
  655.5 0.1 multiply_add_fusion
  655.7 1.9 collective-permute-start.16
  657.6 2.4 collective-permute-start.17
  660.0 2.8 collective-permute-done.17
  662.8 0.1 pad_maximum_fusion
  662.9 0.2 fusion.96
  663.1 1.4 collective-permute-start.18
  664.6 1.3 collective-permute-start.19
  665.9 9.2 %collective-permute-done.18 = f32[4,16,10,1]{3,2,1,0:T(8,128)S(1)} collective-permute-done((f32[4,16,10,1]{3,2,1,0:T(8,128)S(1)}, f32[4,16,10,1]{3,2,1,0:T(8,128)S(1)}, u32[]{:S(2)}, u32[]{:S(2)}) %collective-permute-start.18) | collective-permute-done | bytes 2592 | tf_op jit(solution)/shard_map/ppermute | solution.py:17
  675.0 0.2 fusion.44
  675.3 4.0 collective-permute-done.19
  679.2 0.3 fusion.47
  679.5 0.7 subtract_multiply_fusion
  (40 shorter events, 0.4 us)
Async XLA Ops:
  0.6 0.9 copy-start.1
  1.6 14.7 %copy-start.3 = (s32[16,8,128]{2,1,0:T(8,128)S(1)}, s32[16,8,128]{2,1,0:T(8,128)}, u32[]{:S(2)}) copy-start(s32[16,8,128]{2,1,0:T(8,128)} %param.5) | copy-start | bytes 196612
  1.6 10.3 %copy-start.2 = (f32[16,8,128]{2,1,0:T(8,128)S(1)}, f32[16,8,128]{2,1,0:T(8,128)}, u32[]{:S(2)}) copy-start(f32[16,8,128]{2,1,0:T(8,128)} %param.4) | copy-start | bytes 196612
  1.6 20.3 %collective-permute-start.1 = (f32[2,16,1,128]{3,2,1,0:T(1,128)S(1)}, f32[2,16,1,128]{3,2,1,0:T(1,128)S(1)}, u32[]{:S(2)}, u32[]{:S(2)}) collective-permute-start(f32[2,16,1,128]{3,2,1,0:T(1,128)S(1)} %get-tuple-element.35), channel_id=1, source_target_pairs={{0,16},{16,32},{32,48},{48,64},{64,80},{80,96},{96,112},{112,128},... | collective-permute-start | bytes 49160 | tf_op jit(solution)/shard_map/ppermute | solution.py:17
  6.4 15.6 %collective-permute-start.3 = (f32[2,16,1,128]{3,2,1,0:T(1,128)S(1)}, f32[2,16,1,128]{3,2,1,0:T(1,128)S(1)}, u32[]{:S(2)}, u32[]{:S(2)}) collective-permute-start(f32[2,16,1,128]{3,2,1,0:T(1,128)S(1)} %get-tuple-element.36), channel_id=1, source_target_pairs={{16,0},{32,16},{48,32},{64,48},{80,64},{96,80},{112,96},{128,112},... | collective-permute-start | bytes 49160 | tf_op jit(solution)/shard_map/ppermute | solution.py:18
  11.9 4.5 collective-permute-start
  13.8 5.0 collective-permute-start.2
  18.9 8.7 %collective-permute-start.4 = (f32[16,10,1]{2,1,0:T(8,128)S(1)}, f32[16,10,1]{2,1,0:T(8,128)S(1)}, u32[]{:S(2)}, u32[]{:S(2)}) collective-permute-start(f32[16,10,1]{2,1,0:T(8,128)S(1)} %get-tuple-element.33), channel_id=1, source_target_pairs={{0,1},{1,2},{2,3},{3,4},{4,5},{5,6},{6,7},{7,8},{8,9},{9,10},{10,1... | collective-permute-start | bytes 1928 | tf_op jit(solution)/shard_map/ppermute | solution.py:17
  20.6 7.0 %collective-permute-start.6 = (f32[16,10,1]{2,1,0:T(8,128)S(1)}, f32[16,10,1]{2,1,0:T(8,128)S(1)}, u32[]{:S(2)}, u32[]{:S(2)}) collective-permute-start(f32[16,10,1]{2,1,0:T(8,128)S(1)} %get-tuple-element.34), channel_id=1, source_target_pairs={{1,0},{2,1},{3,2},{4,3},{5,4},{6,5},{7,6},{8,7},{9,8},{10,9},{11,1... | collective-permute-start | bytes 1928 | tf_op jit(solution)/shard_map/ppermute | solution.py:18
  22.1 9.2 %collective-permute-start.5 = (f32[2,16,10,1]{3,2,1,0:T(8,128)S(1)}, f32[2,16,10,1]{3,2,1,0:T(8,128)S(1)}, u32[]{:S(2)}, u32[]{:S(2)}) collective-permute-start(f32[2,16,10,1]{3,2,1,0:T(8,128)S(1)} %get-tuple-element.27), channel_id=1, source_target_pairs={{0,1},{1,2},{2,3},{3,4},{4,5},{5,6},{6,7},{7,8},{8,9},{9,10},{10,1... | collective-permute-start | bytes 3848 | tf_op jit(solution)/shard_map/ppermute | solution.py:17
  26.3 9.2 %collective-permute-start.7 = (f32[2,16,10,1]{3,2,1,0:T(8,128)S(1)}, f32[2,16,10,1]{3,2,1,0:T(8,128)S(1)}, u32[]{:S(2)}, u32[]{:S(2)}) collective-permute-start(f32[2,16,10,1]{3,2,1,0:T(8,128)S(1)} %get-tuple-element.28), channel_id=1, source_target_pairs={{1,0},{2,1},{3,2},{4,3},{5,4},{6,5},{7,6},{8,7},{9,8},{10,9},{11,1... | collective-permute-start | bytes 3848 | tf_op jit(solution)/shard_map/ppermute | solution.py:18
  334.5 4.9 collective-permute-start.8
  337.4 5.1 collective-permute-start.9
  342.7 6.4 collective-permute-start.10
  344.5 8.7 %collective-permute-start.11 = (f32[2,16,10,1]{3,2,1,0:T(8,128)S(1)}, f32[2,16,10,1]{3,2,1,0:T(8,128)S(1)}, u32[]{:S(2)}, u32[]{:S(2)}) collective-permute-start(f32[2,16,10,1]{3,2,1,0:T(8,128)S(1)} %get-tuple-element.26), channel_id=1, source_target_pairs={{1,0},{2,1},{3,2},{4,3},{5,4},{6,5},{7,6},{8,7},{9,8},{10,9},{11,1... | collective-permute-start | bytes 3848 | tf_op jit(solution)/shard_map/ppermute | solution.py:18
  544.1 4.4 collective-permute-start.12
  546.3 5.1 collective-permute-start.13
  551.4 5.2 copy-start.4
  551.5 8.5 %collective-permute-start.14 = (f32[2,16,10,1]{3,2,1,0:T(8,128)S(1)}, f32[2,16,10,1]{3,2,1,0:T(8,128)S(1)}, u32[]{:S(2)}, u32[]{:S(2)}) collective-permute-start(f32[2,16,10,1]{3,2,1,0:T(8,128)S(1)} %get-tuple-element.23), channel_id=1, source_target_pairs={{0,1},{1,2},{2,3},{3,4},{4,5},{5,6},{6,7},{7,8},{8,9},{9,10},{10,1... | collective-permute-start | bytes 3848 | tf_op jit(solution)/shard_map/ppermute | solution.py:17
  555.2 8.9 %collective-permute-start.15 = (f32[2,16,10,1]{3,2,1,0:T(8,128)S(1)}, f32[2,16,10,1]{3,2,1,0:T(8,128)S(1)}, u32[]{:S(2)}, u32[]{:S(2)}) collective-permute-start(f32[2,16,10,1]{3,2,1,0:T(8,128)S(1)} %get-tuple-element.24), channel_id=1, source_target_pairs={{1,0},{2,1},{3,2},{4,3},{5,4},{6,5},{7,6},{8,7},{9,8},{10,9},{11,1... | collective-permute-start | bytes 3848 | tf_op jit(solution)/shard_map/ppermute | solution.py:18
  655.6 23.6 %copy-start = (f32[2,16,8,128]{3,2,1,0:T(8,128)}, f32[2,16,8,128]{3,2,1,0:T(8,128)S(1)}, u32[]{:S(2)}) copy-start(f32[2,16,8,128]{3,2,1,0:T(8,128)S(1)} %multiply_add_fusion) | copy-start | bytes 393220
  655.7 4.4 collective-permute-start.16
  657.6 5.2 collective-permute-start.17
  663.1 11.9 %collective-permute-start.18 = (f32[4,16,10,1]{3,2,1,0:T(8,128)S(1)}, f32[4,16,10,1]{3,2,1,0:T(8,128)S(1)}, u32[]{:S(2)}, u32[]{:S(2)}) collective-permute-start(f32[4,16,10,1]{3,2,1,0:T(8,128)S(1)} %get-tuple-element.19), channel_id=1, source_target_pairs={{0,1},{1,2},{2,3},{3,4},{4,5},{5,6},{6,7},{7,8},{8,9},{9,10},{10,1... | collective-permute-start | bytes 7688 | tf_op jit(solution)/shard_map/ppermute | solution.py:17
  664.6 14.6 %collective-permute-start.19 = (f32[4,16,10,1]{3,2,1,0:T(8,128)S(1)}, f32[4,16,10,1]{3,2,1,0:T(8,128)S(1)}, u32[]{:S(2)}, u32[]{:S(2)}) collective-permute-start(f32[4,16,10,1]{3,2,1,0:T(8,128)S(1)} %get-tuple-element.20), channel_id=1, source_target_pairs={{1,0},{2,1},{3,2},{4,3},{5,4},{6,5},{7,6},{8,7},{9,8},{10,9},{11,1... | collective-permute-start | bytes 7688 | tf_op jit(solution)/shard_map/ppermute | solution.py:18
